TPU v7x, 1024 devices: a whole 4x8x16 slice. The times are simulated.
1024 devices in a mesh: blk: 1024 (over z, x, y, core).
Axes of the slice: x: 4, y: 8, z: 16, core: 2. Of those that a mesh axis runs over, the one named last changes fastest.
Arguments:
- queries: bfloat16 [131072, 512], P('blk'), may hold values from -8 to 8
- key_vectors: bfloat16 [131072, 512], P('blk'), may hold values from -8 to 8
- node_feats: bfloat16 [131072, 512], P('blk'), may hold values from -6 to 6
- w_value: bfloat16 [512, 512], replicated, may hold values from -0.25 to 0.25
- w_out: bfloat16 [512, 512], replicated, may hold values from -0.25 to 0.25
- band_mask: int32 [131072, 640], P('blk'), may hold values 0 or 1
- expander_mask: int32 [131072, 128], P('blk'), may hold values 0 or 1
- partner: int32 [1024], P('blk'), may hold values from 0 to 1023, as said below
- out_grad: bfloat16 [131072, 512], P('blk'), may hold values from -6 to 6
Outputs:
- layer_out: bfloat16 [131072, 512], P('blk')
- query_grad: bfloat16 [131072, 512], P('blk')
- key_grad: bfloat16 [131072, 512], P('blk')
- feature_grad: bfloat16 [131072, 512], P('blk')
Inputs may be any that keep to these rules, and one draw needn't show every extreme that they name: partner[i] is i XOR m for every block i, with one m of 1 to 1023 shared by all blocks.
All inputs are finite; a program needn't handle non-finite values. No bound on the sum of `band_mask` or of `expander_mask` on one device may be relied on, other than what follows from the above.
Results may differ from a plain program's by a relative error of at most 0.007.
Values may be sent and summed in bfloat16 or wider, within the bound.
A program may use at most 32 MiB of HBM per device.

v0:
```python
from functools import partial
import math

import jax
import jax.numpy as jnp
from jax import lax
from jax.sharding import PartitionSpec as P

D = 512
HEADS = 8


cycle_offsets = (-2, -1, 1, 2)


def swapped(block, axis, bit):
    count = lax.axis_size(axis)
    route = []
    for low in range(count):
        high = low | 1 << bit
        if high != low and high < count:
            route += [(low, high), (high, low)]
    return lax.ppermute(block, axis, route)


def passed_along(value, axis, steps):
    count = lax.axis_size(axis)
    pairs = [(source, (source + steps) % count) for source in range(count)]
    return lax.ppermute(value, axis, pairs)


def swap_pair(moved, bit_number):
    arrived = swapped((moved[0], moved[1]), "blk", bit_number)
    return (arrived[0], arrived[1])


def swap_grads(moved, bit_number):
    arrived = swapped((moved[0], moved[1]), "blk", bit_number)
    return (arrived[0], arrived[1])


def keep_pair(moved):
    return (moved[0], moved[1])


def to_partner(moved, match_mask, bit_count, mover):
    moved = (moved[0], moved[1])
    for bit_number in range(bit_count):
        flagged = jnp.bitwise_and(jnp.right_shift(match_mask, bit_number), 1) == 1
        moved = lax.cond(flagged, partial(mover, bit_number=bit_number), keep_pair, moved)
    return moved


def shards(
    queries, key_vectors, node_feats, w_value, w_out, band_mask, expander_mask, partner, out_grad
):
    block_rows = queries.shape[0]
    head_dim = D // HEADS
    scale = 1.0 / math.sqrt(head_dim)
    values = jnp.dot(node_feats, w_value, preferred_element_type=jnp.float32).astype(jnp.bfloat16)
    own_pair = (key_vectors, values)
    fetched = {}
    for offset in cycle_offsets:
        fetched[offset] = passed_along((key_vectors, values), "blk", -offset)
    bit_count = lax.axis_size("blk").bit_length() - 1
    match_mask = jnp.bitwise_xor(partner[0], lax.axis_index("blk"))
    remote = to_partner(own_pair, match_mask, bit_count, swap_pair)
    ordered = [fetched[-2], fetched[-1], own_pair, fetched[1], fetched[2], remote]
    all_keys = jnp.concatenate([key_pair[0] for key_pair in ordered], 0)
    all_values = jnp.concatenate([key_pair[1] for key_pair in ordered], 0)
    key_count = all_keys.shape[0]
    row_ids = lax.broadcasted_iota(jnp.int32, (block_rows, key_count), 0)
    col_ids = lax.broadcasted_iota(jnp.int32, (block_rows, key_count), 1)
    local_col = col_ids - 2 * block_rows
    forced = (local_col == row_ids) | (local_col == jnp.bitwise_xor(row_ids, 1))
    allowed = (jnp.concatenate([band_mask, expander_mask], 1) != 0) | forced
    mask_bias = jnp.where(allowed, 0.0, -jnp.inf).astype(jnp.float32)
    attn_grad = jnp.einsum("re,fe->rf", out_grad, w_out, preferred_element_type=jnp.float32).astype(
        jnp.bfloat16
    )
    group_width = 2 * head_dim
    attended_parts = []
    query_parts = []
    key_parts = []
    value_parts = []
    for head_group in range(HEADS // 2):
        start = head_group * group_width
        finish = start + group_width
        query_heads = queries[:, start:finish].reshape(block_rows, 2, head_dim)
        key_heads = all_keys[:, start:finish].reshape(key_count, 2, head_dim)
        value_heads = all_values[:, start:finish].reshape(key_count, 2, head_dim)
        grad_heads = attn_grad[:, start:finish].reshape(block_rows, 2, head_dim)
        scores = (
            jnp.einsum("rhd,khd->hrk", query_heads, key_heads, preferred_element_type=jnp.float32)
            * scale
            + mask_bias[None]
        )
        row_max = jnp.max(scores, axis=-1, keepdims=True)
        row_total = jnp.sum(jnp.exp(scores - row_max), axis=-1, keepdims=True)
        prob_full = jnp.exp(scores - row_max) / row_total
        prob_half = prob_full.astype(jnp.bfloat16)
        attended_parts.append(
            jnp.einsum("hrk,khd->rhd", prob_half, value_heads, preferred_element_type=jnp.float32)
            .reshape(block_rows, group_width)
            .astype(jnp.bfloat16)
        )
        grad_prob = jnp.einsum(
            "rhd,khd->hrk", grad_heads, value_heads, preferred_element_type=jnp.float32
        )
        row_delta = jnp.sum(prob_full * grad_prob, axis=-1, keepdims=True)
        grad_score = (prob_full * (grad_prob - row_delta) * scale).astype(jnp.bfloat16)
        query_parts.append(
            jnp.einsum("hrk,khd->rhd", grad_score, key_heads, preferred_element_type=jnp.float32)
            .reshape(block_rows, group_width)
            .astype(jnp.bfloat16)
        )
        key_parts.append(
            jnp.einsum("hrk,rhd->khd", grad_score, query_heads, preferred_element_type=jnp.float32)
            .reshape(key_count, group_width)
            .astype(jnp.bfloat16)
        )
        value_parts.append(
            jnp.einsum("hrk,rhd->khd", prob_half, grad_heads, preferred_element_type=jnp.float32)
            .reshape(key_count, group_width)
            .astype(jnp.bfloat16)
        )
    attended = jnp.concatenate(attended_parts, 1)
    layer_out = jnp.dot(attended, w_out, preferred_element_type=jnp.float32).astype(jnp.bfloat16)
    query_grad = jnp.concatenate(query_parts, 1)
    key_terms = jnp.concatenate(key_parts, 1)
    value_terms = jnp.concatenate(value_parts, 1)

    def block_of(terms, slot):
        return terms[slot * block_rows : (slot + 1) * block_rows]

    returned = []
    for offset in cycle_offsets:
        key_send = block_of(key_terms, offset + 2)
        value_send = block_of(value_terms, offset + 2)
        returned.append(passed_along((key_send, value_send), "blk", offset))
    returned.append(
        to_partner(
            (block_of(key_terms, 5), block_of(value_terms, 5)), match_mask, bit_count, swap_grads
        )
    )
    key_sum = block_of(key_terms, 2).astype(jnp.float32)
    value_sum = block_of(value_terms, 2).astype(jnp.float32)
    for arrived in returned:
        key_sum = key_sum + arrived[0].astype(jnp.float32)
        value_sum = value_sum + arrived[1].astype(jnp.float32)
    key_grad = key_sum.astype(jnp.bfloat16)
    value_grad = value_sum.astype(jnp.bfloat16)
    feature_grad = jnp.einsum(
        "rf,ef->re", value_grad, w_value, preferred_element_type=jnp.float32
    ).astype(jnp.bfloat16)
    return (layer_out, query_grad, key_grad, feature_grad)


def solution(mesh):
    placed = (
        P("blk", None),
        P("blk", None),
        P("blk", None),
        P(),
        P(),
        P("blk", None),
        P("blk", None),
        P("blk"),
        P("blk", None),
    )
    return jax.shard_map(
        shards,
        mesh=mesh,
        in_specs=placed,
        out_specs=(P("blk", None), P("blk", None), P("blk", None), P("blk", None)),
        check_vma=False,
    )
```

profile of v0, /device:TPU:1, one launch (start us, length us, event | category | flops | bytes accessed | tf_op | source)
XLA Modules:
  0.0 333.7 jit_solution(7269705596186429427)
XLA Ops:
  2.1 23.9 %collective-permute-start.43 = (bf16[128,512]{1,0:T(8,128)(2,1)S(1)}, bf16[128,512]{1,0:T(8,128)(2,1)S(1)}, u32[]{:S(2)}, u32[]{:S(2)}) collective-permute-start(bf16[128,512]{1,0:T(8,128)(2,1)S(1)} %convolution_convert_fusion.11), channel_id=1, source_target_pairs={{0,1022},{1,1023},{2,0},{3,1},{4,2},{5,3},{6,4},{7,5},{8,6},{9,7},... | collective-permute-start | bytes 393224 | tf_op jit(solution)/shard_map/ppermute | solution.py:29
  33.5 10.9 %conditional.21 = ((bf16[128,512]{1,0:T(8,128)(2,1)}, bf16[128,512]{1,0:T(8,128)(2,1)})) conditional(s32[]{:T(128)} %convert_element_type.283, (bf16[128,512]{1,0:T(8,128)(2,1)}, bf16[128,512]{1,0:T(8,128)(2,1)}) %conditional.20, (bf16[128,512]{1,0:T(8,128)(2,1)}, bf16[128,512]{1,0:T(8,128)(2,1)}) %conditional.20), branch_computations={%region_2.0_spmd, %region_3.0_spmd} | conditional | bytes 1572968 | solution.py:50
  44.4 17.4 %conditional.22 = ((bf16[128,512]{1,0:T(8,128)(2,1)}, bf16[128,512]{1,0:T(8,128)(2,1)})) conditional(s32[]{:T(128)} %convert_element_type.282, (bf16[128,512]{1,0:T(8,128)(2,1)}, bf16[128,512]{1,0:T(8,128)(2,1)}) %get-tuple-element.346, (bf16[128,512]{1,0:T(8,128)(2,1)}, bf16[128,512]{1,0:T(8,128)(2,1)}) %get-tuple-element.346), branch_computations={%region_4.0_spmd, %region_5.0_spmd} | conditional | bytes 1572968 | solution.py:50
  50.6 7.8 %collective-permute-done.4 = bf16[128,512]{1,0:T(8,128)(2,1)S(1)} collective-permute-done((bf16[128,512]{1,0:T(8,128)(2,1)}, bf16[128,512]{1,0:T(8,128)(2,1)S(1)}, u32[]{:S(2)}, u32[]{:S(2)}) %collective-permute-start.4) | collective-permute-done | bytes 131104 | tf_op jit(solution)/shard_map/cond/branch_1_fun/ppermute | solution.py:23
  61.8 10.2 %conditional.24 = ((bf16[128,512]{1,0:T(8,128)(2,1)}, bf16[128,512]{1,0:T(8,128)(2,1)})) conditional(s32[]{:T(128)} %convert_element_type.280, (bf16[128,512]{1,0:T(8,128)(2,1)}, bf16[128,512]{1,0:T(8,128)(2,1)}) %get-tuple-element.348, (bf16[128,512]{1,0:T(8,128)(2,1)}, bf16[128,512]{1,0:T(8,128)(2,1)}) %get-tuple-element.348), branch_computations={%region_8.0_spmd, %region_9.0_spmd} | conditional | bytes 1572968 | solution.py:50
  72.0 11.7 %conditional.25 = ((bf16[128,512]{1,0:T(8,128)(2,1)}, bf16[128,512]{1,0:T(8,128)(2,1)})) conditional(s32[]{:T(128)} %convert_element_type.279, (bf16[128,512]{1,0:T(8,128)(2,1)}, bf16[128,512]{1,0:T(8,128)(2,1)}) %get-tuple-element.349, (bf16[128,512]{1,0:T(8,128)(2,1)}, bf16[128,512]{1,0:T(8,128)(2,1)}) %get-tuple-element.349), branch_computations={%region_10.0_spmd, %region_11.0_spmd} | conditional | bytes 1572968 | solution.py:50
  83.7 11.1 %conditional.27 = ((bf16[128,512]{1,0:T(8,128)(2,1)}, bf16[128,512]{1,0:T(8,128)(2,1)})) conditional(s32[]{:T(128)} %convert_element_type.277, (bf16[128,512]{1,0:T(8,128)(2,1)}, bf16[128,512]{1,0:T(8,128)(2,1)}) %get-tuple-element.351, (bf16[128,512]{1,0:T(8,128)(2,1)}, bf16[128,512]{1,0:T(8,128)(2,1)}) %get-tuple-element.351), branch_computations={%region_14.0_spmd, %region_15.0_spmd} | conditional | bytes 1572968 | solution.py:50
  94.7 25.5 %conditional.28 = ((bf16[128,512]{1,0:T(8,128)(2,1)}, bf16[128,512]{1,0:T(8,128)(2,1)})) conditional(s32[]{:T(128)} %convert_element_type.276, (bf16[128,512]{1,0:T(8,128)(2,1)}, bf16[128,512]{1,0:T(8,128)(2,1)}) %get-tuple-element.352, (bf16[128,512]{1,0:T(8,128)(2,1)}, bf16[128,512]{1,0:T(8,128)(2,1)}) %get-tuple-element.352), branch_computations={%region_16.0_spmd, %region_17.0_spmd} | conditional | bytes 1572968 | solution.py:50
  96.6 7.3 %collective-permute-start.17 = (bf16[128,512]{1,0:T(8,128)(2,1)}, bf16[128,512]{1,0:T(8,128)(2,1)S(1)}, u32[]{:S(2)}, u32[]{:S(2)}) collective-permute-start(bf16[128,512]{1,0:T(8,128)(2,1)} %get-tuple-element.189), channel_id=1, source_target_pairs={{0,256},{256,0},{1,257},{257,1},{2,258},{258,2},{3,259},{259,3},{4... | collective-permute-start | bytes 393224 | tf_op jit(solution)/shard_map/cond/branch_1_fun/ppermute | solution.py:23
  103.9 12.9 %collective-permute-done.16 = bf16[128,512]{1,0:T(8,128)(2,1)S(1)} collective-permute-done((bf16[128,512]{1,0:T(8,128)(2,1)}, bf16[128,512]{1,0:T(8,128)(2,1)S(1)}, u32[]{:S(2)}, u32[]{:S(2)}) %collective-permute-start.16) | collective-permute-done | bytes 131104 | tf_op jit(solution)/shard_map/cond/branch_1_fun/ppermute | solution.py:23
  129.3 9.5 %collective-permute-done.44 = bf16[128,512]{1,0:T(8,128)(2,1)S(1)} collective-permute-done((bf16[128,512]{1,0:T(8,128)(2,1)S(1)}, bf16[128,512]{1,0:T(8,128)(2,1)S(1)}, u32[]{:S(2)}, u32[]{:S(2)}) %collective-permute-start.44) | collective-permute-done | bytes 131104 | tf_op jit(solution)/shard_map/ppermute | solution.py:29
  143.8 6.2 %collective-permute-done.40 = bf16[128,512]{1,0:T(8,128)(2,1)S(1)} collective-permute-done((bf16[128,512]{1,0:T(8,128)(2,1)S(1)}, bf16[128,512]{1,0:T(8,128)(2,1)S(1)}, u32[]{:S(2)}, u32[]{:S(2)}) %collective-permute-start.40) | collective-permute-done | bytes 131104 | tf_op jit(solution)/shard_map/ppermute | solution.py:29
  195.1 8.3 %collective-permute-start.52 = (bf16[128,512]{1,0:T(8,128)(2,1)}, bf16[128,512]{1,0:T(8,128)(2,1)}, u32[]{:S(2)}, u32[]{:S(2)}) collective-permute-start(bf16[128,512]{1,0:T(8,128)(2,1)} %get-tuple-element.230), channel_id=1, source_target_pairs={{0,1022},{1,1023},{2,0},{3,1},{4,2},{5,3},{6,4},{7,5},{8,6},{9,7},... | collective-permute-start | bytes 393224 | tf_op jit(solution)/shard_map/ppermute | solution.py:29
  208.1 8.8 %conditional.31 = ((bf16[128,512]{1,0:T(8,128)(2,1)S(1)}, bf16[128,512]{1,0:T(8,128)(2,1)S(1)})) conditional(s32[]{:T(128)} %convert_element_type.283, (bf16[128,512]{1,0:T(8,128)(2,1)S(1)}, bf16[128,512]{1,0:T(8,128)(2,1)S(1)}) %get-tuple-element.355, (bf16[128,512]{1,0:T(8,128)(2,1)S(1)}, bf16[128,512]{1,0:T(8,128)(2,1)S(1)}) %get-tuple-element.355), branch_computations={%region_34.35_spmd, %region_35.36_spmd} | conditional | bytes 1572968 | solution.py:50
  216.9 15.3 %conditional.32 = ((bf16[128,512]{1,0:T(8,128)(2,1)S(1)}, bf16[128,512]{1,0:T(8,128)(2,1)S(1)})) conditional(s32[]{:T(128)} %convert_element_type.282, (bf16[128,512]{1,0:T(8,128)(2,1)S(1)}, bf16[128,512]{1,0:T(8,128)(2,1)S(1)}) %get-tuple-element.356, (bf16[128,512]{1,0:T(8,128)(2,1)S(1)}, bf16[128,512]{1,0:T(8,128)(2,1)S(1)}) %get-tuple-element.356), branch_computations={%region_36.37_spmd, %region_37.38_spmd} | conditional | bytes 1572968 | solution.py:50
  226.3 5.9 %collective-permute-done.25 = bf16[128,512]{1,0:T(8,128)(2,1)S(1)} collective-permute-done((bf16[128,512]{1,0:T(8,128)(2,1)S(1)}, bf16[128,512]{1,0:T(8,128)(2,1)S(1)}, u32[]{:S(2)}, u32[]{:S(2)}) %collective-permute-start.25) | collective-permute-done | bytes 131104 | tf_op jit(solution)/shard_map/cond/branch_1_fun/ppermute | solution.py:23
  232.2 9.1 %conditional.34 = ((bf16[128,512]{1,0:T(8,128)(2,1)S(1)}, bf16[128,512]{1,0:T(8,128)(2,1)S(1)})) conditional(s32[]{:T(128)} %convert_element_type.280, (bf16[128,512]{1,0:T(8,128)(2,1)S(1)}, bf16[128,512]{1,0:T(8,128)(2,1)S(1)}) %get-tuple-element.358, (bf16[128,512]{1,0:T(8,128)(2,1)S(1)}, bf16[128,512]{1,0:T(8,128)(2,1)S(1)}) %get-tuple-element.358), branch_computations={%region_40.41_spmd, %region_41.42_spmd} | conditional | bytes 1572968 | solution.py:50
  241.3 10.3 %conditional.35 = ((bf16[128,512]{1,0:T(8,128)(2,1)S(1)}, bf16[128,512]{1,0:T(8,128)(2,1)S(1)})) conditional(s32[]{:T(128)} %convert_element_type.279, (bf16[128,512]{1,0:T(8,128)(2,1)S(1)}, bf16[128,512]{1,0:T(8,128)(2,1)S(1)}) %get-tuple-element.359, (bf16[128,512]{1,0:T(8,128)(2,1)S(1)}, bf16[128,512]{1,0:T(8,128)(2,1)S(1)}) %get-tuple-element.359), branch_computations={%region_42.43_spmd, %region_43.44_spmd} | conditional | bytes 1572968 | solution.py:50
  243.3 4.9 %collective-permute-start.31 = (bf16[128,512]{1,0:T(8,128)(2,1)S(1)}, bf16[128,512]{1,0:T(8,128)(2,1)S(1)}, u32[]{:S(2)}, u32[]{:S(2)}) collective-permute-start(bf16[128,512]{1,0:T(8,128)(2,1)S(1)} %get-tuple-element.203), channel_id=1, source_target_pairs={{0,32},{32,0},{1,33},{33,1},{2,34},{34,2},{3,35},{35,3},{4,36},{36... | collective-permute-start | bytes 393224 | tf_op jit(solution)/shard_map/cond/branch_1_fun/ppermute | solution.py:23
  251.7 9.4 %conditional.37 = ((bf16[128,512]{1,0:T(8,128)(2,1)S(1)}, bf16[128,512]{1,0:T(8,128)(2,1)S(1)})) conditional(s32[]{:T(128)} %convert_element_type.277, (bf16[128,512]{1,0:T(8,128)(2,1)S(1)}, bf16[128,512]{1,0:T(8,128)(2,1)S(1)}) %get-tuple-element.361, (bf16[128,512]{1,0:T(8,128)(2,1)S(1)}, bf16[128,512]{1,0:T(8,128)(2,1)S(1)}) %get-tuple-element.361), branch_computations={%region_46.47_spmd, %region_47.48_spmd} | conditional | bytes 1572968 | solution.py:50
  261.1 27.3 %conditional.38 = ((bf16[128,512]{1,0:T(8,128)(2,1)S(1)}, bf16[128,512]{1,0:T(8,128)(2,1)S(1)})) conditional(s32[]{:T(128)} %convert_element_type.276, (bf16[128,512]{1,0:T(8,128)(2,1)S(1)}, bf16[128,512]{1,0:T(8,128)(2,1)S(1)}) %get-tuple-element.362, (bf16[128,512]{1,0:T(8,128)(2,1)S(1)}, bf16[128,512]{1,0:T(8,128)(2,1)S(1)}) %get-tuple-element.362), branch_computations={%region_48.49_spmd, %region_49.50_spmd} | conditional | bytes 1572968 | solution.py:50
  263.5 6.8 %collective-permute-start.37 = (bf16[128,512]{1,0:T(8,128)(2,1)S(1)}, bf16[128,512]{1,0:T(8,128)(2,1)S(1)}, u32[]{:S(2)}, u32[]{:S(2)}) collective-permute-start(bf16[128,512]{1,0:T(8,128)(2,1)S(1)} %get-tuple-element.209), channel_id=1, source_target_pairs={{0,256},{256,0},{1,257},{257,1},{2,258},{258,2},{3,259},{259,3},{4... | collective-permute-start | bytes 393224 | tf_op jit(solution)/shard_map/cond/branch_1_fun/ppermute | solution.py:23
  270.3 15.2 %collective-permute-done.36 = bf16[128,512]{1,0:T(8,128)(2,1)S(1)} collective-permute-done((bf16[128,512]{1,0:T(8,128)(2,1)S(1)}, bf16[128,512]{1,0:T(8,128)(2,1)S(1)}, u32[]{:S(2)}, u32[]{:S(2)}) %collective-permute-start.36) | collective-permute-done | bytes 131104 | tf_op jit(solution)/shard_map/cond/branch_1_fun/ppermute | solution.py:23
  290.7 22.4 %collective-permute-start.48 = (bf16[128,512]{1,0:T(8,128)(2,1)}, bf16[128,512]{1,0:T(8,128)(2,1)}, u32[]{:S(2)}, u32[]{:S(2)}) collective-permute-start(bf16[128,512]{1,0:T(8,128)(2,1)} %get-tuple-element.235), channel_id=1, source_target_pairs={{0,1022},{1,1023},{2,0},{3,1},{4,2},{5,3},{6,4},{7,5},{8,6},{9,7},... | collective-permute-start | bytes 393224 | tf_op jit(solution)/shard_map/ppermute | solution.py:29
  (223 shorter events, 201.4 us)
Async XLA Ops:
  2.1 153.7 %collective-permute-start.43 = (bf16[128,512]{1,0:T(8,128)(2,1)S(1)}, bf16[128,512]{1,0:T(8,128)(2,1)S(1)}, u32[]{:S(2)}, u32[]{:S(2)}) collective-permute-start(bf16[128,512]{1,0:T(8,128)(2,1)S(1)} %convolution_convert_fusion.11), channel_id=1, source_target_pairs={{0,1022},{1,1023},{2,0},{3,1},{4,2},{5,3},{6,4},{7,5},{8,6},{9,7},... | collective-permute-start | bytes 393224 | tf_op jit(solution)/shard_map/ppermute | solution.py:29
  25.9 129.8 %collective-permute-start.42 = (bf16[128,512]{1,0:T(8,128)(2,1)S(1)}, bf16[128,512]{1,0:T(8,128)(2,1)S(1)}, u32[]{:S(2)}, u32[]{:S(2)}) collective-permute-start(bf16[128,512]{1,0:T(8,128)(2,1)S(1)} %convolution_convert_fusion.11), channel_id=1, source_target_pairs={{0,1023},{1,0},{2,1},{3,2},{4,3},{5,4},{6,5},{7,6},{8,7},{9,8},{10... | collective-permute-start | bytes 393224 | tf_op jit(solution)/shard_map/ppermute | solution.py:29
  28.8 124.3 %collective-permute-start.41 = (bf16[128,512]{1,0:T(8,128)(2,1)S(1)}, bf16[128,512]{1,0:T(8,128)(2,1)S(1)}, u32[]{:S(2)}, u32[]{:S(2)}) collective-permute-start(bf16[128,512]{1,0:T(8,128)(2,1)S(1)} %convolution_convert_fusion.11), channel_id=1, source_target_pairs={{0,1},{1,2},{2,3},{3,4},{4,5},{5,6},{6,7},{7,8},{8,9},{9,10},{10,1... | collective-permute-start | bytes 393224 | tf_op jit(solution)/shard_map/ppermute | solution.py:29
  44.4 13.9 %collective-permute-start.4 = (bf16[128,512]{1,0:T(8,128)(2,1)}, bf16[128,512]{1,0:T(8,128)(2,1)S(1)}, u32[]{:S(2)}, u32[]{:S(2)}) collective-permute-start(bf16[128,512]{1,0:T(8,128)(2,1)} %get-tuple-element.176), channel_id=1, source_target_pairs={{0,4},{4,0},{1,5},{5,1},{2,6},{6,2},{3,7},{7,3},{8,12},{12,8},{9,1... | collective-permute-start | bytes 393224 | tf_op jit(solution)/shard_map/cond/branch_1_fun/ppermute | solution.py:23
  46.3 14.8 %collective-permute-start.5 = (bf16[128,512]{1,0:T(8,128)(2,1)}, bf16[128,512]{1,0:T(8,128)(2,1)S(1)}, u32[]{:S(2)}, u32[]{:S(2)}) collective-permute-start(bf16[128,512]{1,0:T(8,128)(2,1)} %get-tuple-element.177), channel_id=1, source_target_pairs={{0,4},{4,0},{1,5},{5,1},{2,6},{6,2},{3,7},{7,3},{8,12},{12,8},{9,1... | collective-permute-start | bytes 393224 | tf_op jit(solution)/shard_map/cond/branch_1_fun/ppermute | solution.py:23
  73.9 9.1 %collective-permute-start.11 = (bf16[128,512]{1,0:T(8,128)(2,1)}, bf16[128,512]{1,0:T(8,128)(2,1)S(1)}, u32[]{:S(2)}, u32[]{:S(2)}) collective-permute-start(bf16[128,512]{1,0:T(8,128)(2,1)} %get-tuple-element.183), channel_id=1, source_target_pairs={{0,32},{32,0},{1,33},{33,1},{2,34},{34,2},{3,35},{35,3},{4,36},{36... | collective-permute-start | bytes 393224 | tf_op jit(solution)/shard_map/cond/branch_1_fun/ppermute | solution.py:23
  85.7 8.4 %collective-permute-start.15 = (bf16[128,512]{1,0:T(8,128)(2,1)}, bf16[128,512]{1,0:T(8,128)(2,1)S(1)}, u32[]{:S(2)}, u32[]{:S(2)}) collective-permute-start(bf16[128,512]{1,0:T(8,128)(2,1)} %get-tuple-element.187), channel_id=1, source_target_pairs={{0,128},{128,0},{1,129},{129,1},{2,130},{130,2},{3,131},{131,3},{4... | collective-permute-start | bytes 393224 | tf_op jit(solution)/shard_map/cond/branch_1_fun/ppermute | solution.py:23
  94.7 22.0 %collective-permute-start.16 = (bf16[128,512]{1,0:T(8,128)(2,1)}, bf16[128,512]{1,0:T(8,128)(2,1)S(1)}, u32[]{:S(2)}, u32[]{:S(2)}) collective-permute-start(bf16[128,512]{1,0:T(8,128)(2,1)} %get-tuple-element.188), channel_id=1, source_target_pairs={{0,256},{256,0},{1,257},{257,1},{2,258},{258,2},{3,259},{259,3},{4... | collective-permute-start | bytes 393224 | tf_op jit(solution)/shard_map/cond/branch_1_fun/ppermute | solution.py:23
  96.6 22.9 %collective-permute-start.17 = (bf16[128,512]{1,0:T(8,128)(2,1)}, bf16[128,512]{1,0:T(8,128)(2,1)S(1)}, u32[]{:S(2)}, u32[]{:S(2)}) collective-permute-start(bf16[128,512]{1,0:T(8,128)(2,1)} %get-tuple-element.189), channel_id=1, source_target_pairs={{0,256},{256,0},{1,257},{257,1},{2,258},{258,2},{3,259},{259,3},{4... | collective-permute-start | bytes 393224 | tf_op jit(solution)/shard_map/cond/branch_1_fun/ppermute | solution.py:23
  120.2 20.6 %collective-permute-start.45 = (bf16[128,512]{1,0:T(8,128)(2,1)S(1)}, bf16[128,512]{1,0:T(8,128)(2,1)S(1)}, u32[]{:S(2)}, u32[]{:S(2)}) collective-permute-start(bf16[128,512]{1,0:T(8,128)(2,1)S(1)} %copy-done.3), channel_id=1, source_target_pairs={{0,1},{1,2},{2,3},{3,4},{4,5},{5,6},{6,7},{7,8},{8,9},{9,10},{10,1... | collective-permute-start | bytes 393224 | tf_op jit(solution)/shard_map/ppermute | solution.py:29
  122.3 16.6 %collective-permute-start.44 = (bf16[128,512]{1,0:T(8,128)(2,1)S(1)}, bf16[128,512]{1,0:T(8,128)(2,1)S(1)}, u32[]{:S(2)}, u32[]{:S(2)}) collective-permute-start(bf16[128,512]{1,0:T(8,128)(2,1)S(1)} %copy-done.3), channel_id=1, source_target_pairs={{0,2},{1,3},{2,4},{3,5},{4,6},{5,7},{6,8},{7,9},{8,10},{9,11},{10,... | collective-permute-start | bytes 393224 | tf_op jit(solution)/shard_map/ppermute | solution.py:29
  138.9 11.1 %collective-permute-start.40 = (bf16[128,512]{1,0:T(8,128)(2,1)S(1)}, bf16[128,512]{1,0:T(8,128)(2,1)S(1)}, u32[]{:S(2)}, u32[]{:S(2)}) collective-permute-start(bf16[128,512]{1,0:T(8,128)(2,1)S(1)} %convolution_convert_fusion.11), channel_id=1, source_target_pairs={{0,2},{1,3},{2,4},{3,5},{4,6},{5,7},{6,8},{7,9},{8,10},{9,11},{10,... | collective-permute-start | bytes 393224 | tf_op jit(solution)/shard_map/ppermute | solution.py:29
  140.8 12.3 %collective-permute-start.46 = (bf16[128,512]{1,0:T(8,128)(2,1)S(1)}, bf16[128,512]{1,0:T(8,128)(2,1)S(1)}, u32[]{:S(2)}, u32[]{:S(2)}) collective-permute-start(bf16[128,512]{1,0:T(8,128)(2,1)S(1)} %copy-done.3), channel_id=1, source_target_pairs={{0,1023},{1,0},{2,1},{3,2},{4,3},{5,4},{6,5},{7,6},{8,7},{9,8},{10... | collective-permute-start | bytes 393224 | tf_op jit(solution)/shard_map/ppermute | solution.py:29
  195.1 124.6 %collective-permute-start.52 = (bf16[128,512]{1,0:T(8,128)(2,1)}, bf16[128,512]{1,0:T(8,128)(2,1)}, u32[]{:S(2)}, u32[]{:S(2)}) collective-permute-start(bf16[128,512]{1,0:T(8,128)(2,1)} %get-tuple-element.230), channel_id=1, source_target_pairs={{0,1022},{1,1023},{2,0},{3,1},{4,2},{5,3},{6,4},{7,5},{8,6},{9,7},... | collective-permute-start | bytes 393224 | tf_op jit(solution)/shard_map/ppermute | solution.py:29
  203.4 118.2 %collective-permute-start.55 = (bf16[128,512]{1,0:T(8,128)(2,1)}, bf16[128,512]{1,0:T(8,128)(2,1)}, u32[]{:S(2)}, u32[]{:S(2)}) collective-permute-start(bf16[128,512]{1,0:T(8,128)(2,1)} %get-tuple-element.231), channel_id=1, source_target_pairs={{0,2},{1,3},{2,4},{3,5},{4,6},{5,7},{6,8},{7,9},{8,10},{9,11},{10,... | collective-permute-start | bytes 393224 | tf_op jit(solution)/shard_map/ppermute | solution.py:29
  205.3 119.8 %collective-permute-start.54 = (bf16[128,512]{1,0:T(8,128)(2,1)}, bf16[128,512]{1,0:T(8,128)(2,1)}, u32[]{:S(2)}, u32[]{:S(2)}) collective-permute-start(bf16[128,512]{1,0:T(8,128)(2,1)} %get-tuple-element.232), channel_id=1, source_target_pairs={{0,1},{1,2},{2,3},{3,4},{4,5},{5,6},{6,7},{7,8},{8,9},{9,10},{10,1... | collective-permute-start | bytes 393224 | tf_op jit(solution)/shard_map/ppermute | solution.py:29
  216.9 9.4 %collective-permute-start.24 = (bf16[128,512]{1,0:T(8,128)(2,1)S(1)}, bf16[128,512]{1,0:T(8,128)(2,1)S(1)}, u32[]{:S(2)}, u32[]{:S(2)}) collective-permute-start(bf16[128,512]{1,0:T(8,128)(2,1)S(1)} %get-tuple-element.196), channel_id=1, source_target_pairs={{0,4},{4,0},{1,5},{5,1},{2,6},{6,2},{3,7},{7,3},{8,12},{12,8},{9,1... | collective-permute-start | bytes 393224 | tf_op jit(solution)/shard_map/cond/branch_1_fun/ppermute | solution.py:23
  218.8 13.4 %collective-permute-start.25 = (bf16[128,512]{1,0:T(8,128)(2,1)S(1)}, bf16[128,512]{1,0:T(8,128)(2,1)S(1)}, u32[]{:S(2)}, u32[]{:S(2)}) collective-permute-start(bf16[128,512]{1,0:T(8,128)(2,1)S(1)} %get-tuple-element.197), channel_id=1, source_target_pairs={{0,4},{4,0},{1,5},{5,1},{2,6},{6,2},{3,7},{7,3},{8,12},{12,8},{9,1... | collective-permute-start | bytes 393224 | tf_op jit(solution)/shard_map/cond/branch_1_fun/ppermute | solution.py:23
  261.1 24.4 %collective-permute-start.36 = (bf16[128,512]{1,0:T(8,128)(2,1)S(1)}, bf16[128,512]{1,0:T(8,128)(2,1)S(1)}, u32[]{:S(2)}, u32[]{:S(2)}) collective-permute-start(bf16[128,512]{1,0:T(8,128)(2,1)S(1)} %get-tuple-element.208), channel_id=1, source_target_pairs={{0,256},{256,0},{1,257},{257,1},{2,258},{258,2},{3,259},{259,3},{4... | collective-permute-start | bytes 393224 | tf_op jit(solution)/shard_map/cond/branch_1_fun/ppermute | solution.py:23
  263.5 24.8 %collective-permute-start.37 = (bf16[128,512]{1,0:T(8,128)(2,1)S(1)}, bf16[128,512]{1,0:T(8,128)(2,1)S(1)}, u32[]{:S(2)}, u32[]{:S(2)}) collective-permute-start(bf16[128,512]{1,0:T(8,128)(2,1)S(1)} %get-tuple-element.209), channel_id=1, source_target_pairs={{0,256},{256,0},{1,257},{257,1},{2,258},{258,2},{3,259},{259,3},{4... | collective-permute-start | bytes 393224 | tf_op jit(solution)/shard_map/cond/branch_1_fun/ppermute | solution.py:23
  288.3 39.1 %collective-permute-start.53 = (bf16[128,512]{1,0:T(8,128)(2,1)S(1)}, bf16[128,512]{1,0:T(8,128)(2,1)}, u32[]{:S(2)}, u32[]{:S(2)}) collective-permute-start(bf16[128,512]{1,0:T(8,128)(2,1)S(1)} %get-tuple-element.233), channel_id=1, source_target_pairs={{0,1023},{1,0},{2,1},{3,2},{4,3},{5,4},{6,5},{7,6},{8,7},{9,8},{10... | collective-permute-start | bytes 393224 | tf_op jit(solution)/shard_map/ppermute | solution.py:29
  290.7 38.8 %collective-permute-start.48 = (bf16[128,512]{1,0:T(8,128)(2,1)}, bf16[128,512]{1,0:T(8,128)(2,1)}, u32[]{:S(2)}, u32[]{:S(2)}) collective-permute-start(bf16[128,512]{1,0:T(8,128)(2,1)} %get-tuple-element.235), channel_id=1, source_target_pairs={{0,1022},{1,1023},{2,0},{3,1},{4,2},{5,3},{6,4},{7,5},{8,6},{9,7},... | collective-permute-start | bytes 393224 | tf_op jit(solution)/shard_map/ppermute | solution.py:29
  319.7 12.3 %collective-permute-start.51 = (bf16[128,512]{1,0:T(8,128)(2,1)}, bf16[128,512]{1,0:T(8,128)(2,1)S(1)}, u32[]{:S(2)}, u32[]{:S(2)}) collective-permute-start(bf16[128,512]{1,0:T(8,128)(2,1)} %get-tuple-element.237), channel_id=1, source_target_pairs={{0,2},{1,3},{2,4},{3,5},{4,6},{5,7},{6,8},{7,9},{8,10},{9,11},{10,... | collective-permute-start | bytes 393224 | tf_op jit(solution)/shard_map/ppermute | solution.py:29
  321.6 10.4 %collective-permute-start.50 = (bf16[128,512]{1,0:T(8,128)(2,1)S(1)}, bf16[128,512]{1,0:T(8,128)(2,1)S(1)}, u32[]{:S(2)}, u32[]{:S(2)}) collective-permute-start(bf16[128,512]{1,0:T(8,128)(2,1)S(1)} %get-tuple-element.238), channel_id=1, source_target_pairs={{0,1},{1,2},{2,3},{3,4},{4,5},{5,6},{6,7},{7,8},{8,9},{9,10},{10,1... | collective-permute-start | bytes 393224 | tf_op jit(solution)/shard_map/ppermute | solution.py:29
  (36 other events, 593.7 us)
where the time goes:
time: 336 us; the launch traced here: 334 us
  starting transfers between devices  164 us (49%)
  waiting for transfers between devices  101 us (30%)
  matrix products  40.8 us (12%)
  local copies, waits for them, and re-layouts  21.8 us (6%)
    ppermute x16, starting transfers between devices, passed_along(): return lax.ppermute(value, axis, pairs)  86.5 us
    ppermute x24, waiting for transfers between devices, swapped(): return lax.ppermute(block, axis, route)  80.5 us
    ppermute x24, starting transfers between devices, swapped(): return lax.ppermute(block, axis, route)  77.9 us
    ppermute x16, waiting for transfers between devices, passed_along(): return lax.ppermute(value, axis, pairs)  20.9 us
    cond x26, local copies, waits for them, and re-layouts  9.17 us
    dot_general x4, matrix products, shards(): jnp.einsum('hrk,rhd->khd', grad_score, query_heads, preferred_element_typ...  8.14 us
    dot_general x4, matrix products, shards(): jnp.einsum('hrk,khd->rhd', grad_score, key_heads, preferred_element_type=...  7.68 us
  transfers between devices with their start and end apart: 40, of which 28 were waited for; matrix products, arithmetic and copies ran while one was open for 7% of the time, Pallas kernels for 0%

commit v1 on v0

v1 whole, which is shorter than its diff:
```python
from functools import partial
import math

import jax
import jax.numpy as jnp
from jax import lax
from jax.experimental import pallas as pl
from jax.experimental.pallas import tpu as pltpu
from jax.sharding import PartitionSpec as P

D = 512
HEADS = 8
ROWS = 128
GROUP = 128
LOW = 64
CYCLE = (-2, -1, 1, 2)
MESH = pl.DeviceIdType.MESH
BF16 = jnp.bfloat16
F32 = jnp.float32
PAIR = jax.ShapeDtypeStruct((2, ROWS, D), BF16)
RING = jax.ShapeDtypeStruct((4, 2, ROWS, D), BF16)
NT = (((1,), (1,)), ((), ()))
TN = (((0,), (0,)), ((), ()))


def greet(peers):
    barrier = pltpu.get_barrier_semaphore()
    for peer in peers:
        pl.semaphore_signal(barrier, inc=1, device_id=(peer,), device_id_type=MESH)
    pl.semaphore_wait(barrier, len(peers))


def swap_kernel(mask, pair_ref, out_ref, send, recv):
    peer = jnp.bitwise_xor(lax.axis_index("blk"), mask)
    greet([peer])
    copy = pltpu.make_async_remote_copy(
        pair_ref, out_ref, send, recv, device_id=(peer,), device_id_type=MESH
    )
    copy.start()
    copy.wait()


def swap_low(pair, match_mask, low, first_id):
    def branch(mask):
        if mask == 0:
            return lambda block: block
        return pl.pallas_call(
            partial(swap_kernel, mask),
            out_shape=PAIR,
            in_specs=[pl.BlockSpec(memory_space=pl.ANY)],
            out_specs=pl.BlockSpec(memory_space=pl.ANY),
            scratch_shapes=[pltpu.SemaphoreType.DMA, pltpu.SemaphoreType.DMA],
            compiler_params=pltpu.CompilerParams(
                collective_id=first_id + mask, has_side_effects=True
            ),
        )

    return lax.switch(match_mask % low, [branch(mask) for mask in range(low)], pair)


def ring_kernel(mask, count, spread, *refs):
    if mask:
        pair_ref, ring_ref, pair_out, ring_out, send, recv = refs
    else:
        ring_ref, ring_out, send, recv = refs
    me = lax.axis_index("blk")
    peers = [lax.rem(me + offset + count, count) for offset in CYCLE]
    far = jnp.bitwise_xor(me, mask)
    greet(peers + ([far] if mask else []))
    copies = []
    if mask:
        copies.append(
            pltpu.make_async_remote_copy(
                pair_ref, pair_out, send.at[4], recv.at[4], device_id=(far,), device_id_type=MESH
            )
        )
    for slot, peer in enumerate(peers):
        source = ring_ref.at[slot] if spread else ring_ref
        copies.append(
            pltpu.make_async_remote_copy(
                source,
                ring_out.at[3 - slot],
                send.at[slot],
                recv.at[3 - slot],
                device_id=(peer,),
                device_id_type=MESH,
            )
        )
    for copy in copies:
        copy.start()
    for copy in copies:
        copy.wait_send()
    for copy in copies:
        copy.wait_recv()


def swap_high(pair, ring, match_mask, low, first_id):
    count = lax.axis_size("blk")
    spread = ring.ndim == 4

    def branch(high):
        call = pl.pallas_call(
            partial(ring_kernel, high * low, count, spread),
            out_shape=(PAIR, RING) if high else RING,
            in_specs=[pl.BlockSpec(memory_space=pl.ANY)] * (2 if high else 1),
            out_specs=(pl.BlockSpec(memory_space=pl.ANY),) * 2
            if high
            else pl.BlockSpec(memory_space=pl.ANY),
            scratch_shapes=[pltpu.SemaphoreType.DMA((5,)), pltpu.SemaphoreType.DMA((5,))],
            compiler_params=pltpu.CompilerParams(
                collective_id=first_id + high, has_side_effects=True
            ),
        )
        return call if high else lambda pair, ring: (pair, call(ring))

    return lax.switch(
        match_mask // low, [branch(high) for high in range(count // low)], pair, ring
    )


def project_kernel(feats_ref, weight_ref, keys_ref, pair_ref):
    pair_ref[0] = keys_ref[...]
    pair_ref[1] = jnp.dot(
        feats_ref[...], weight_ref[...], preferred_element_type=F32
    ).astype(BF16)


def attend_kernel(
    query_ref, own_ref, ring_ref, match_ref, band_ref, expander_ref, cot_ref, weight_ref,
    layer_ref, dquery_ref, own_out, ring_out, match_out, bias_ref, grad_ref, att_ref,
):
    rate = 1.0 / math.sqrt(D // HEADS)
    rate2 = rate * math.log2(math.e)
    row = lax.broadcasted_iota(jnp.int32, (ROWS, ROWS), 0)
    col = lax.broadcasted_iota(jnp.int32, (ROWS, ROWS), 1)
    for slot in range(6):
        edges = expander_ref[...] if slot == 5 else band_ref[:, slot * ROWS : (slot + 1) * ROWS]
        allowed = edges != 0
        if slot == 2:
            allowed = allowed | (col == row) | (col == jnp.bitwise_xor(row, 1))
        bias_ref[slot] = jnp.where(allowed, 0.0, -jnp.inf).astype(F32).T
    grad_ref[...] = lax.dot_general(
        cot_ref[...], weight_ref[...], NT, preferred_element_type=F32
    ).astype(BF16)
    lane = lax.broadcasted_iota(jnp.int32, (ROWS, GROUP), 1)
    zero = jnp.zeros((ROWS, GROUP), BF16)

    def stacked(block):
        return jnp.concatenate(
            [jnp.where(lane < 64, block, zero), jnp.where(lane < 64, zero, block)], 0
        )

    def unstacked(block):
        return jnp.concatenate([block[:64, :ROWS], block[64:, ROWS:]], 0)

    sources = [ring_ref.at[0], ring_ref.at[1], own_ref, ring_ref.at[2], ring_ref.at[3], match_ref]
    targets = [ring_out.at[0], ring_out.at[1], own_out, ring_out.at[2], ring_out.at[3], match_out]
    for group in range(D // GROUP):
        lanes = slice(group * GROUP, (group + 1) * GROUP)
        queries = stacked(query_ref[:, lanes])
        grads = stacked(grad_ref[:, lanes])
        scores = []
        for slot in range(6):
            bias = bias_ref[slot]
            product = lax.dot_general(
                sources[slot][0, :, lanes], queries, NT, preferred_element_type=F32
            )
            scores.append(product * rate2 + jnp.concatenate([bias, bias], 1))
        top = jnp.max(
            jnp.maximum(
                jnp.maximum(jnp.maximum(scores[0], scores[1]), jnp.maximum(scores[2], scores[3])),
                jnp.maximum(scores[4], scores[5]),
            ),
            axis=0,
            keepdims=True,
        )
        weights = [jnp.exp2(score - top) for score in scores]
        total = jnp.sum(
            (weights[0] + weights[1]) + (weights[2] + weights[3]) + (weights[4] + weights[5]),
            axis=0,
            keepdims=True,
        )
        inverse = 1.0 / total
        probs = [weight * inverse for weight in weights]
        halves = [prob.astype(BF16) for prob in probs]
        attended = jnp.zeros((GROUP, 2 * ROWS), F32)
        products = []
        running = jnp.zeros((ROWS, 2 * ROWS), F32)
        for slot in range(6):
            value = sources[slot][1, :, lanes]
            attended += lax.dot_general(value, halves[slot], TN, preferred_element_type=F32)
            targets[slot][1, :, lanes] = jnp.dot(
                halves[slot], grads, preferred_element_type=F32
            ).astype(BF16)
            grad_prob = lax.dot_general(value, grads, NT, preferred_element_type=F32)
            products.append(grad_prob)
            running += probs[slot] * grad_prob
        att_ref[lanes, :] = unstacked(attended).astype(BF16)
        delta = jnp.sum(running, axis=0, keepdims=True)
        dquery = jnp.zeros((GROUP, 2 * ROWS), F32)
        for slot in range(6):
            grad_score = (probs[slot] * (products[slot] - delta) * rate).astype(BF16)
            dquery += lax.dot_general(
                sources[slot][0, :, lanes], grad_score, TN, preferred_element_type=F32
            )
            targets[slot][0, :, lanes] = jnp.dot(
                grad_score, queries, preferred_element_type=F32
            ).astype(BF16)
        dquery_ref[:, lanes] = unstacked(dquery).T.astype(BF16)
    layer_ref[...] = lax.dot_general(
        att_ref[...], weight_ref[...], TN, preferred_element_type=F32
    ).astype(BF16)


def combine_kernel(own_ref, ring_ref, match_ref, weight_ref, key_ref, feature_ref):
    key_sum = own_ref[0].astype(F32)
    value_sum = own_ref[1].astype(F32)
    for slot in range(4):
        key_sum += ring_ref[slot, 0].astype(F32)
        value_sum += ring_ref[slot, 1].astype(F32)
    key_ref[...] = (key_sum + match_ref[0].astype(F32)).astype(BF16)
    value_grad = (value_sum + match_ref[1].astype(F32)).astype(BF16)
    feature_ref[...] = lax.dot_general(
        value_grad, weight_ref[...], NT, preferred_element_type=F32
    ).astype(BF16)


def shards(
    queries, key_vectors, node_feats, w_value, w_out, band_mask, expander_mask, partner, out_grad
):
    count = lax.axis_size("blk")
    low = min(LOW, count // 2)
    ids = [1, 1 + low, 1 + low + count // low, 1 + 2 * low + count // low]
    plain = jax.ShapeDtypeStruct((ROWS, D), BF16)
    roomy = pltpu.CompilerParams(vmem_limit_bytes=48 << 20)
    match_mask = jnp.bitwise_xor(partner[0], lax.axis_index("blk"))
    own = pl.pallas_call(project_kernel, out_shape=PAIR, compiler_params=roomy)(
        node_feats, w_value, key_vectors
    )
    near = swap_low(own, match_mask, low, ids[0])
    match, ring = swap_high(near, own, match_mask, low, ids[1])
    layer_out, query_grad, own_terms, ring_terms, match_terms = pl.pallas_call(
        attend_kernel,
        out_shape=(plain, plain, PAIR, RING, PAIR),
        scratch_shapes=[
            pltpu.VMEM((6, ROWS, ROWS), F32),
            pltpu.VMEM((ROWS, D), BF16),
            pltpu.VMEM((D, ROWS), BF16),
        ],
        compiler_params=roomy,
    )(queries, own, ring, match, band_mask, expander_mask, out_grad, w_out)
    near_terms, ring_back = swap_high(match_terms, ring_terms, match_mask, low, ids[2])
    match_back = swap_low(near_terms, match_mask, low, ids[3])
    key_grad, feature_grad = pl.pallas_call(
        combine_kernel, out_shape=(plain, plain), compiler_params=roomy
    )(own_terms, ring_back, match_back, w_value)
    return (layer_out, query_grad, key_grad, feature_grad)


def solution(mesh):
    rows = P("blk", None)
    return jax.shard_map(
        shards,
        mesh=mesh,
        in_specs=(rows, rows, rows, P(), P(), rows, rows, P("blk"), rows),
        out_specs=(rows, rows, rows, rows),
        check_vma=False,
    )
```

time: 336 us -> 215 us (0.64)
  Pallas kernels: 0 us -> 208 us
  starting transfers between devices: 164 us -> 0 us
  waiting for transfers between devices: 101 us -> 0 us
  matrix products: 40.8 us -> 0 us
  local copies, waits for them, and re-layouts: 21.8 us -> 5 us
    pallas_call x0 -> x7, Pallas kernels: none -> 208 us  [the longest x2 128 us: swap_high(): lax.switch(match_mask // low, [branch(high) for high in range(count // lo...]
    ppermute x40 -> x0, starting transfers between devices: 164 us -> none  [the longest x16 86.5 us: passed_along(): return lax.ppermute(value, axis, pairs)]
    ppermute x40 -> x0, waiting for transfers between devices: 101 us -> none  [the longest x24 80.5 us: swapped(): return lax.ppermute(block, axis, route)]
    dot_general x24 -> x0, matrix products: 35.6 us -> none  [the longest x4 8.14 us: shards(): jnp.einsum('hrk,rhd->khd', grad_score, query_heads, preferred_element_typ...]
    cond x26 -> x3, local copies, waits for them, and re-layouts: 9.17 us -> 2.12 us
    slice x22 -> x0, local copies, waits for them, and re-layouts: 6.35 us -> none  [the longest x5 1.72 us: shards(): query_heads = queries[:, start:finish].reshape(block_rows, 2, head_dim)]
    sub x4 -> x0, matrix products: 5.16 us -> none  [shards(): prob_full = jnp.exp(scores - row_max) / row_total]
  transfers between devices with their start and end apart: 40 -> 0, of which waited for: 28 -> 0; matrix products, arithmetic and copies ran while one was open for 7% -> 0% of each run, Pallas kernels for 0% -> 0%
where the time goes in v1:
time: 215 us; the launch traced here: 214 us
  Pallas kernels  208 us (97%)
  local copies, waits for them, and re-layouts  5 us (2%)
    pallas_call x2, Pallas kernels, swap_high(): lax.switch(match_mask // low, [branch(high) for high in range(count // lo...  128 us
    pallas_call x2, Pallas kernels, swap_low(): lax.switch(match_mask % low, [branch(mask) for mask in range(low)], pair)  71.8 us
    pallas_call x1, Pallas kernels, shards(): pl.pallas_call(attend_kernel, out_shape=(plain, plain, PAIR, RING, PAIR),...  6.69 us

profile of v1, /device:TPU:1, one launch (start us, length us, event | category | flops | bytes accessed | tf_op | source)
XLA Modules:
  0.0 214.4 jit_solution(5909943594188550896)
XLA Ops:
  1.3 0.0 copy-start
  1.3 1.0 copy-done
  2.4 0.9 copy-done.4
  3.3 0.9 copy-done.5
  4.2 0.2 shard_map.120.own_ref
  4.4 45.5 %conditional.4 = (bf16[2,128,512]{2,1,0:T(8,128)(2,1)S(1)}) conditional(s32[]{:T(128)} %clamp.9, bf16[2,128,512]{2,1,0:T(8,128)(2,1)S(1)} %shard_map.120.own_ref, bf16[2,128,512]{2,1,0:T(8,128)(2,1)S(1)} %shard_map.120.own_ref, bf16[2,128,512]{2,1,0:T(8,128)(2,1)S(1)} %shard_map.120.own_ref, ...), branch_computations={%region_0.1_spmd, %region_1.2_spmd, %region_2.3_spmd, %region_3.4_... | conditional | bytes 524296 | solution.py:58
  4.5 45.5 %branch_45_fun.2 = bf16[2,128,512]{2,1,0:T(8,128)(2,1)S(1)} custom-call(bf16[2,128,512]{2,1,0:T(8,128)(2,1)S(1)} %pair_ref.44), custom_call_target="tpu_custom_call" | custom-call | tf_op jit(solution)/shard_map/cond/branch_45_fun/pallas_call | solution.py:58
  50.0 0.0 copy-start.2
  50.0 0.0 copy-start.3
  50.0 0.0 copy-start.6
  50.0 0.0 copy-start.7
  50.0 0.0 copy-start.8
  50.0 72.2 %conditional.5 = ((bf16[2,128,512]{2,1,0:T(8,128)(2,1)S(1)}, bf16[4,2,128,512]{3,2,1,0:T(8,128)(2,1)})) conditional(s32[]{:T(128)} %clamp.8, (bf16[2,128,512]{2,1,0:T(8,128)(2,1)S(1)}, bf16[2,128,512]{2,1,0:T(8,128)(2,1)S(1)}) %tuple.490, (bf16[2,128,512]{2,1,0:T(8,128)(2,1)S(1)}, ...), branch_computations={%region_64.65_spmd, %region_65.66_spmd, %region_66.67_spmd, %regio... | conditional | bytes 524296 | solution.py:116
  50.1 0.7 copy.313.refs_0_
  50.8 71.4 %branch_15_fun.5 = (bf16[2,128,512]{2,1,0:T(8,128)(2,1)S(1)}, bf16[4,2,128,512]{3,2,1,0:T(8,128)(2,1)}) custom-call(bf16[2,128,512]{2,1,0:T(8,128)(2,1)} %copy.313.refs_0_, bf16[2,128,512]{2,1,0:T(8,128)(2,1)S(1)} %get-tuple-element.417.refs_1_), custom_call_target="tpu_custom_call" | custom-call | tf_op jit(solution)/shard_map/cond/branch_15_fun/pallas_call | solution.py:116
  122.2 6.7 %shard_map.121 = (bf16[128,512]{1,0:T(8,128)(2,1)}, bf16[128,512]{1,0:T(8,128)(2,1)}, bf16[2,128,512]{2,1,0:T(8,128)(2,1)S(1)}, bf16[4,2,128,512]{3,2,1,0:T(8,128)(2,1)S(1)}, bf16[2,128,512]{2,1,0:T(8,128)(2,1)S(1)}) custom-call(bf16[128,512]{1,0:T(8,128)(2,1)S(1)} %copy-done.6, bf16[2,128,512]{2,1,0:T(8,128)(2,1)S(1)} %shard_map.120.own_ref, ...), custom_call_target="tpu_custom_call" | custom-call | tf_op jit(solution)/shard_map/pallas_call | solution.py:242
  128.9 57.2 %conditional.6 = ((bf16[2,128,512]{2,1,0:T(8,128)(2,1)S(1)}, bf16[4,2,128,512]{3,2,1,0:T(8,128)(2,1)S(1)})) conditional(s32[]{:T(128)} %clamp.8, (bf16[4,2,128,512]{3,2,1,0:T(8,128)(2,1)S(1)}, bf16[2,128,512]{2,1,0:T(8,128)(2,1)S(1)}) %tuple.492, (bf16[2,128,512]{2,1,0:T(8,128)(2,1)S(1)}, ...), branch_computations={%region_80.81_spmd, %region_81.82_spmd, %region_82.83_spmd, %regio... | conditional | bytes 524296 | solution.py:116
  128.9 0.7 copy.328.refs_0_
  129.6 56.5 %branch_15_fun.6 = (bf16[2,128,512]{2,1,0:T(8,128)(2,1)S(1)}, bf16[4,2,128,512]{3,2,1,0:T(8,128)(2,1)S(1)}) custom-call(bf16[2,128,512]{2,1,0:T(8,128)(2,1)} %copy.328.refs_0_, bf16[4,2,128,512]{3,2,1,0:T(8,128)(2,1)S(1)} %get-tuple-element.449.refs_1_), custom_call_target="tpu_custom_call" | custom-call | tf_op jit(solution)/shard_map/cond/branch_15_fun/pallas_call | solution.py:116
  186.2 0.0 copy-start.1
  186.2 27.1 %conditional.7 = (bf16[2,128,512]{2,1,0:T(8,128)(2,1)S(1)}) conditional(s32[]{:T(128)} %clamp.9, bf16[2,128,512]{2,1,0:T(8,128)(2,1)S(1)} %get-tuple-element.473, bf16[2,128,512]{2,1,0:T(8,128)(2,1)S(1)} %get-tuple-element.473, bf16[2,128,512]{2,1,0:T(8,128)(2,1)S(1)} %get-tuple-element.473, ...), branch_computations={%region_96.97_spmd, %region_97.98_spmd, %region_98.99_spmd, %regio... | conditional | bytes 524296 | solution.py:58
  186.3 0.7 copy.373.pair_ref
  187.0 26.3 %branch_45_fun.3 = bf16[2,128,512]{2,1,0:T(8,128)(2,1)S(1)} custom-call(bf16[2,128,512]{2,1,0:T(8,128)(2,1)} %copy.373.pair_ref), custom_call_target="tpu_custom_call" | custom-call | tf_op jit(solution)/shard_map/cond/branch_45_fun/pallas_call | solution.py:58
  213.3 1.0 shard_map.122
  (8 shorter events, 0.0 us)
Async XLA Ops:
  1.3 1.0 copy-start
  2.4 0.9 copy-start.4
  3.3 0.9 copy-start.5
  50.0 72.2 %copy-start.2 = (bf16[512,512]{1,0:T(8,128)(2,1)S(1)}, bf16[512,512]{1,0:T(8,128)(2,1)}, u32[]{:S(2)}) copy-start(bf16[512,512]{1,0:T(8,128)(2,1)} %weight_ref.4) | copy-start | bytes 1572868
  50.0 72.2 %copy-start.3 = (s32[128,640]{1,0:T(8,128)S(1)}, s32[128,640]{1,0:T(8,128)}, u32[]{:S(2)}) copy-start(s32[128,640]{1,0:T(8,128)} %band_ref.1) | copy-start | bytes 983044
  50.0 72.2 %copy-start.6 = (bf16[128,512]{1,0:T(8,128)(2,1)S(1)}, bf16[128,512]{1,0:T(8,128)(2,1)}, u32[]{:S(2)}) copy-start(bf16[128,512]{1,0:T(8,128)(2,1)} %query_ref.1) | copy-start | bytes 393220
  50.0 72.2 %copy-start.7 = (bf16[128,512]{1,0:T(8,128)(2,1)S(1)}, bf16[128,512]{1,0:T(8,128)(2,1)}, u32[]{:S(2)}) copy-start(bf16[128,512]{1,0:T(8,128)(2,1)} %cot_ref.1) | copy-start | bytes 393220
  50.0 72.2 %copy-start.8 = (s32[128,128]{1,0:T(8,128)S(1)}, s32[128,128]{1,0:T(8,128)}, u32[]{:S(2)}) copy-start(s32[128,128]{1,0:T(8,128)} %expander_ref.1) | copy-start | bytes 196612
  186.2 27.1 %copy-start.1 = (bf16[512,512]{1,0:T(8,128)(2,1)S(1)}, bf16[512,512]{1,0:T(8,128)(2,1)}, u32[]{:S(2)}) copy-start(bf16[512,512]{1,0:T(8,128)(2,1)} %weight_ref.5) | copy-start | bytes 1572868

commit v2 on v1

--- a/solution.py
+++ b/solution.py
@@ -12,6 +12,7 @@
 HEADS = 8
 ROWS = 128
 GROUP = 128
+SWAPS = ((16, 4), (1, 16))
 LOW = 64
 CYCLE = (-2, -1, 1, 2)
 MESH = pl.DeviceIdType.MESH
@@ -33,32 +34,37 @@
 def swap_kernel(mask, pair_ref, out_ref, send, recv):
     peer = jnp.bitwise_xor(lax.axis_index("blk"), mask)
     greet([peer])
-    copy = pltpu.make_async_remote_copy(
-        pair_ref, out_ref, send, recv, device_id=(peer,), device_id_type=MESH
-    )
-    copy.start()
-    copy.wait()
-
-
-def swap_low(pair, match_mask, low, first_id):
-    def branch(mask):
-        if mask == 0:
-            return lambda block: block
-        return pl.pallas_call(
-            partial(swap_kernel, mask),
-            out_shape=PAIR,
-            in_specs=[pl.BlockSpec(memory_space=pl.ANY)],
-            out_specs=pl.BlockSpec(memory_space=pl.ANY),
-            scratch_shapes=[pltpu.SemaphoreType.DMA, pltpu.SemaphoreType.DMA],
-            compiler_params=pltpu.CompilerParams(
-                collective_id=first_id + mask, has_side_effects=True
-            ),
-        )
-
-    return lax.switch(match_mask % low, [branch(mask) for mask in range(low)], pair)
-
-
-def ring_kernel(mask, count, spread, *refs):
+    copies = [
+        pltpu.make_async_remote_copy(
+            pair_ref.at[half],
+            out_ref.at[half],
+            send.at[half],
+            recv.at[half],
+            device_id=(peer,),
+            device_id_type=MESH,
+        )
+        for half in range(2)
+    ]
+    for copy in copies:
+        copy.start()
+    for copy in copies:
+        copy.wait()
+
+
+def swap(mask, first_id, pair):
+    if mask == 0:
+        return pair
+    return pl.pallas_call(
+        partial(swap_kernel, mask),
+        out_shape=PAIR,
+        in_specs=[pl.BlockSpec(memory_space=pl.ANY)],
+        out_specs=pl.BlockSpec(memory_space=pl.ANY),
+        scratch_shapes=[pltpu.SemaphoreType.DMA((2,)), pltpu.SemaphoreType.DMA((2,))],
+        compiler_params=pltpu.CompilerParams(collective_id=first_id, has_side_effects=True),
+    )(pair)
+
+
+def ring_kernel(mask, count, *refs):
     if mask:
         pair_ref, ring_ref, pair_out, ring_out, send, recv = refs
     else:
@@ -69,16 +75,21 @@
     greet(peers + ([far] if mask else []))
     copies = []
     if mask:
+        for half in range(2):
+            copies.append(
+                pltpu.make_async_remote_copy(
+                    pair_ref.at[half],
+                    pair_out.at[half],
+                    send.at[4 + half],
+                    recv.at[4 + half],
+                    device_id=(far,),
+                    device_id_type=MESH,
+                )
+            )
+    for slot, peer in enumerate(peers):
         copies.append(
             pltpu.make_async_remote_copy(
-                pair_ref, pair_out, send.at[4], recv.at[4], device_id=(far,), device_id_type=MESH
-            )
-        )
-    for slot, peer in enumerate(peers):
-        source = ring_ref.at[slot] if spread else ring_ref
-        copies.append(
-            pltpu.make_async_remote_copy(
-                source,
+                ring_ref.at[slot],
                 ring_out.at[3 - slot],
                 send.at[slot],
                 recv.at[3 - slot],
@@ -94,35 +105,41 @@
         copy.wait_recv()
 
 
-def swap_high(pair, ring, match_mask, low, first_id):
+def swap_ring(mask, first_id, count, pair, ring):
+    call = pl.pallas_call(
+        partial(ring_kernel, mask, count),
+        out_shape=(PAIR, RING) if mask else RING,
+        in_specs=[pl.BlockSpec(memory_space=pl.ANY)] * (2 if mask else 1),
+        out_specs=(pl.BlockSpec(memory_space=pl.ANY),) * 2
+        if mask
+        else pl.BlockSpec(memory_space=pl.ANY),
+        scratch_shapes=[pltpu.SemaphoreType.DMA((6,)), pltpu.SemaphoreType.DMA((6,))],
+        compiler_params=pltpu.CompilerParams(collective_id=first_id, has_side_effects=True),
+    )
+    return call(pair, ring) if mask else (pair, call(ring))
+
+
+def travel(pair, ring, match_mask):
     count = lax.axis_size("blk")
-    spread = ring.ndim == 4
-
-    def branch(high):
-        call = pl.pallas_call(
-            partial(ring_kernel, high * low, count, spread),
-            out_shape=(PAIR, RING) if high else RING,
-            in_specs=[pl.BlockSpec(memory_space=pl.ANY)] * (2 if high else 1),
-            out_specs=(pl.BlockSpec(memory_space=pl.ANY),) * 2
-            if high
-            else pl.BlockSpec(memory_space=pl.ANY),
-            scratch_shapes=[pltpu.SemaphoreType.DMA((5,)), pltpu.SemaphoreType.DMA((5,))],
-            compiler_params=pltpu.CompilerParams(
-                collective_id=first_id + high, has_side_effects=True
-            ),
-        )
-        return call if high else lambda pair, ring: (pair, call(ring))
-
-    return lax.switch(
-        match_mask // low, [branch(high) for high in range(count // low)], pair, ring
-    )
-
-
-def project_kernel(feats_ref, weight_ref, keys_ref, pair_ref):
-    pair_ref[0] = keys_ref[...]
-    pair_ref[1] = jnp.dot(
-        feats_ref[...], weight_ref[...], preferred_element_type=F32
-    ).astype(BF16)
+    first_id = 0
+    for unit, size in SWAPS:
+        branches = [partial(swap, part * unit, first_id + part - 1) for part in range(size)]
+        first_id += size - 1
+        pair = lax.switch(match_mask // unit % size, branches, pair)
+    branches = [
+        partial(swap_ring, part * LOW, first_id + part, count) for part in range(count // LOW)
+    ]
+    return lax.switch(match_mask // LOW, branches, pair, ring)
+
+
+def project_kernel(feats_ref, weight_ref, keys_ref, pair_ref, ring_ref):
+    keys = keys_ref[...]
+    values = jnp.dot(feats_ref[...], weight_ref[...], preferred_element_type=F32).astype(BF16)
+    pair_ref[0] = keys
+    pair_ref[1] = values
+    for slot in range(4):
+        ring_ref[slot, 0] = keys
+        ring_ref[slot, 1] = values
 
 
 def attend_kernel(
@@ -228,32 +245,30 @@
 def shards(
     queries, key_vectors, node_feats, w_value, w_out, band_mask, expander_mask, partner, out_grad
 ):
-    count = lax.axis_size("blk")
-    low = min(LOW, count // 2)
-    ids = [1, 1 + low, 1 + low + count // low, 1 + 2 * low + count // low]
     plain = jax.ShapeDtypeStruct((ROWS, D), BF16)
     roomy = pltpu.CompilerParams(vmem_limit_bytes=48 << 20)
     match_mask = jnp.bitwise_xor(partner[0], lax.axis_index("blk"))
-    own = pl.pallas_call(project_kernel, out_shape=PAIR, compiler_params=roomy)(
-        node_feats, w_value, key_vectors
-    )
-    near = swap_low(own, match_mask, low, ids[0])
-    match, ring = swap_high(near, own, match_mask, low, ids[1])
-    layer_out, query_grad, own_terms, ring_terms, match_terms = pl.pallas_call(
-        attend_kernel,
-        out_shape=(plain, plain, PAIR, RING, PAIR),
-        scratch_shapes=[
-            pltpu.VMEM((6, ROWS, ROWS), F32),
-            pltpu.VMEM((ROWS, D), BF16),
-            pltpu.VMEM((D, ROWS), BF16),
-        ],
-        compiler_params=roomy,
-    )(queries, own, ring, match, band_mask, expander_mask, out_grad, w_out)
-    near_terms, ring_back = swap_high(match_terms, ring_terms, match_mask, low, ids[2])
-    match_back = swap_low(near_terms, match_mask, low, ids[3])
+    own, spread = pl.pallas_call(
+        project_kernel, out_shape=(PAIR, RING), compiler_params=roomy
+    )(node_feats, w_value, key_vectors)
+    pair, ring = own, spread
+    for backward in (False, True):
+        pair, ring = travel(pair, ring, match_mask)
+        if backward:
+            break
+        layer_out, query_grad, own_terms, ring, pair = pl.pallas_call(
+            attend_kernel,
+            out_shape=(plain, plain, PAIR, RING, PAIR),
+            scratch_shapes=[
+                pltpu.VMEM((6, ROWS, ROWS), F32),
+                pltpu.VMEM((ROWS, D), BF16),
+                pltpu.VMEM((D, ROWS), BF16),
+            ],
+            compiler_params=roomy,
+        )(queries, own, ring, pair, band_mask, expander_mask, out_grad, w_out)
     key_grad, feature_grad = pl.pallas_call(
         combine_kernel, out_shape=(plain, plain), compiler_params=roomy
-    )(own_terms, ring_back, match_back, w_value)
+    )(own_terms, ring, pair, w_value)
     return (layer_out, query_grad, key_grad, feature_grad)
 
 

time: 215 us -> 132 us (0.61)
  the two profiles are of different devices: /device:TPU:1 before, /device:TPU:257 now
where the time goes in v2:
time: 132 us
  Pallas kernels  124 us (94%)
  local copies, waits for them, and re-layouts  6.37 us (5%)
  between operations  1.5 us (1%)
    pallas_call x2, Pallas kernels, swap_ring(): return call(pair, ring) if mask else (pair, call(ring))  75.7 us
    pallas_call x4, Pallas kernels, swap(): pl.pallas_call(partial(swap_kernel, mask), out_shape=PAIR, in_specs=[pl.B...  40.2 us
    pallas_call x1, Pallas kernels, shards(): pl.pallas_call(attend_kernel, out_shape=(plain, plain, PAIR, RING, PAIR),...  6.68 us
    cond x5, local copies, waits for them, and re-layouts  3.49 us
    unnamed x18, local copies, waits for them, and re-layouts  2.88 us

profile of v2, /device:TPU:257, one launch (start us, length us, event | category | flops | bytes accessed | tf_op | source)
XLA Modules:
  0.0 132.0 jit_solution(13860097436746948133)
XLA Ops:
  1.3 0.0 copy-start
  1.4 1.0 copy-done
  2.4 0.9 copy-done.4
  3.3 0.9 copy-done.5
  4.2 0.2 shard_map.120
  4.4 8.0 %conditional.6 = (bf16[2,128,512]{2,1,0:T(8,128)(2,1)S(1)}) conditional(s32[]{:T(128)} %clamp.14, bf16[2,128,512]{2,1,0:T(8,128)(2,1)S(1)} %get-tuple-element.293.own_ref, bf16[2,128,512]{2,1,0:T(8,128)(2,1)S(1)} %get-tuple-element.293.own_ref, bf16[2,128,512]{2,1,0:T(8,128)(2,1)S(1)} %get-tuple-element.293.own_ref, ...), branch_computations={%region_0.1_spmd, %region_1.2_spmd, %region_2.3_spmd, %region_3.4_... | conditional | bytes 524296 | solution.py:128
  4.5 7.9 %branch_1_fun.6 = bf16[2,128,512]{2,1,0:T(8,128)(2,1)S(1)} custom-call(bf16[2,128,512]{2,1,0:T(8,128)(2,1)S(1)} %pair_ref), custom_call_target="tpu_custom_call" | custom-call | tf_op jit(solution)/shard_map/cond/branch_1_fun/pallas_call | solution.py:57
  12.4 15.8 %conditional.7 = (bf16[2,128,512]{2,1,0:T(8,128)(2,1)S(1)}) conditional(s32[]{:T(128)} %clamp.13, bf16[2,128,512]{2,1,0:T(8,128)(2,1)S(1)} %get-tuple-element.370, bf16[2,128,512]{2,1,0:T(8,128)(2,1)S(1)} %get-tuple-element.370, bf16[2,128,512]{2,1,0:T(8,128)(2,1)S(1)} %get-tuple-element.370, ...), branch_computations={%region_4.5_spmd, %region_5.6_spmd, %region_6.7_spmd, %region_7.8_... | conditional | bytes 524296 | solution.py:128
  12.5 0.7 copy.194.pair_ref
  13.2 15.1 %branch_14_fun.4 = bf16[2,128,512]{2,1,0:T(8,128)(2,1)S(1)} custom-call(bf16[2,128,512]{2,1,0:T(8,128)(2,1)} %copy.194.pair_ref), custom_call_target="tpu_custom_call" | custom-call | tf_op jit(solution)/shard_map/cond/branch_14_fun/pallas_call | solution.py:57
  28.4 42.6 %conditional.8 = ((bf16[2,128,512]{2,1,0:T(8,128)(2,1)S(1)}, bf16[4,2,128,512]{3,2,1,0:T(8,128)(2,1)})) conditional(s32[]{:T(128)} %clamp.12, (bf16[4,2,128,512]{3,2,1,0:T(8,128)(2,1)S(1)}, bf16[2,128,512]{2,1,0:T(8,128)(2,1)S(1)}) %tuple.226, (bf16[2,128,512]{2,1,0:T(8,128)(2,1)S(1)}, ...), branch_computations={%region_20.21_spmd, %region_21.22_spmd, %region_22.23_spmd, %regio... | conditional | bytes 524296 | solution.py:132
  28.4 0.7 copy.200.refs_0_
  29.1 41.8 %branch_5_fun.5 = (bf16[2,128,512]{2,1,0:T(8,128)(2,1)S(1)}, bf16[4,2,128,512]{3,2,1,0:T(8,128)(2,1)}) custom-call(bf16[2,128,512]{2,1,0:T(8,128)(2,1)} %copy.200.refs_0_, bf16[4,2,128,512]{3,2,1,0:T(8,128)(2,1)S(1)} %get-tuple-element.223.refs_1_), custom_call_target="tpu_custom_call" | custom-call | tf_op jit(solution)/shard_map/cond/branch_5_fun/pallas_call | solution.py:119
  71.0 6.7 %shard_map.121 = (bf16[128,512]{1,0:T(8,128)(2,1)}, bf16[128,512]{1,0:T(8,128)(2,1)}, bf16[2,128,512]{2,1,0:T(8,128)(2,1)S(1)}, bf16[4,2,128,512]{3,2,1,0:T(8,128)(2,1)S(1)}, bf16[2,128,512]{2,1,0:T(8,128)(2,1)S(1)}) custom-call(bf16[128,512]{1,0:T(8,128)(2,1)S(1)} %copy-done.6, bf16[2,128,512]{2,1,0:T(8,128)(2,1)S(1)} %get-tuple-element.293.own_ref, ...), custom_call_target="tpu_custom_call" | custom-call | tf_op jit(solution)/shard_map/pallas_call | solution.py:259
  77.6 8.2 %conditional.9 = (bf16[2,128,512]{2,1,0:T(8,128)(2,1)S(1)}) conditional(s32[]{:T(128)} %clamp.14, bf16[2,128,512]{2,1,0:T(8,128)(2,1)S(1)} %get-tuple-element.301, bf16[2,128,512]{2,1,0:T(8,128)(2,1)S(1)} %get-tuple-element.301, bf16[2,128,512]{2,1,0:T(8,128)(2,1)S(1)} %get-tuple-element.301, ...), branch_computations={%region_36.37_spmd, %region_37.38_spmd, %region_38.39_spmd, %regio... | conditional | bytes 524296 | solution.py:128
  77.6 0.7 copy.211.pair_ref
  78.3 7.4 %branch_1_fun.9 = bf16[2,128,512]{2,1,0:T(8,128)(2,1)S(1)} custom-call(bf16[2,128,512]{2,1,0:T(8,128)(2,1)} %copy.211.pair_ref), custom_call_target="tpu_custom_call" | custom-call | tf_op jit(solution)/shard_map/cond/branch_1_fun/pallas_call | solution.py:57
  85.8 10.5 %conditional.10 = (bf16[2,128,512]{2,1,0:T(8,128)(2,1)S(1)}) conditional(s32[]{:T(128)} %clamp.13, bf16[2,128,512]{2,1,0:T(8,128)(2,1)S(1)} %get-tuple-element.373, bf16[2,128,512]{2,1,0:T(8,128)(2,1)S(1)} %get-tuple-element.373, bf16[2,128,512]{2,1,0:T(8,128)(2,1)S(1)} %get-tuple-element.373, ...), branch_computations={%region_40.41_spmd, %region_41.42_spmd, %region_42.43_spmd, %regio... | conditional | bytes 524296 | solution.py:128
  85.9 0.7 copy.227.pair_ref
  86.6 9.7 %branch_14_fun.6 = bf16[2,128,512]{2,1,0:T(8,128)(2,1)S(1)} custom-call(bf16[2,128,512]{2,1,0:T(8,128)(2,1)} %copy.227.pair_ref), custom_call_target="tpu_custom_call" | custom-call | tf_op jit(solution)/shard_map/cond/branch_14_fun/pallas_call | solution.py:57
  96.3 34.6 %conditional.11 = ((bf16[2,128,512]{2,1,0:T(8,128)(2,1)S(1)}, bf16[4,2,128,512]{3,2,1,0:T(8,128)(2,1)S(1)})) conditional(s32[]{:T(128)} %clamp.12, (bf16[4,2,128,512]{3,2,1,0:T(8,128)(2,1)S(1)}, bf16[2,128,512]{2,1,0:T(8,128)(2,1)S(1)}) %tuple.228, (bf16[2,128,512]{2,1,0:T(8,128)(2,1)S(1)}, ...), branch_computations={%region_56.57_spmd, %region_57.58_spmd, %region_58.59_spmd, %regio... | conditional | bytes 524296 | solution.py:132
  96.4 0.7 copy.233.refs_0_
  97.1 33.9 %branch_5_fun.7 = (bf16[2,128,512]{2,1,0:T(8,128)(2,1)S(1)}, bf16[4,2,128,512]{3,2,1,0:T(8,128)(2,1)S(1)}) custom-call(bf16[2,128,512]{2,1,0:T(8,128)(2,1)} %copy.233.refs_0_, bf16[4,2,128,512]{3,2,1,0:T(8,128)(2,1)S(1)} %get-tuple-element.255.refs_1_), custom_call_target="tpu_custom_call" | custom-call | tf_op jit(solution)/shard_map/cond/branch_5_fun/pallas_call | solution.py:119
  131.0 1.0 shard_map.122
  (14 shorter events, 0.0 us)
Async XLA Ops:
  1.3 1.0 copy-start
  2.4 0.9 copy-start.4
  3.3 0.9 copy-start.5
  28.3 42.6 %copy-start.2 = (bf16[512,512]{1,0:T(8,128)(2,1)S(1)}, bf16[512,512]{1,0:T(8,128)(2,1)}, u32[]{:S(2)}) copy-start(bf16[512,512]{1,0:T(8,128)(2,1)} %weight_ref.4) | copy-start | bytes 1572868
  28.3 42.6 %copy-start.3 = (s32[128,640]{1,0:T(8,128)S(1)}, s32[128,640]{1,0:T(8,128)}, u32[]{:S(2)}) copy-start(s32[128,640]{1,0:T(8,128)} %band_ref.1) | copy-start | bytes 983044
  28.3 42.6 %copy-start.6 = (bf16[128,512]{1,0:T(8,128)(2,1)S(1)}, bf16[128,512]{1,0:T(8,128)(2,1)}, u32[]{:S(2)}) copy-start(bf16[128,512]{1,0:T(8,128)(2,1)} %query_ref.1) | copy-start | bytes 393220
  28.3 42.6 %copy-start.7 = (bf16[128,512]{1,0:T(8,128)(2,1)S(1)}, bf16[128,512]{1,0:T(8,128)(2,1)}, u32[]{:S(2)}) copy-start(bf16[128,512]{1,0:T(8,128)(2,1)} %cot_ref.1) | copy-start | bytes 393220
  28.3 42.6 %copy-start.8 = (s32[128,128]{1,0:T(8,128)S(1)}, s32[128,128]{1,0:T(8,128)}, u32[]{:S(2)}) copy-start(s32[128,128]{1,0:T(8,128)} %expander_ref.1) | copy-start | bytes 196612
  96.3 34.6 %copy-start.1 = (bf16[512,512]{1,0:T(8,128)(2,1)S(1)}, bf16[512,512]{1,0:T(8,128)(2,1)}, u32[]{:S(2)}) copy-start(bf16[512,512]{1,0:T(8,128)(2,1)} %weight_ref.5) | copy-start | bytes 1572868
